TPU v7x, 512 devices: a whole 4x8x8 slice. The times are simulated.
512 devices in a mesh: dom: 32 (over y, x_hi, core), band: 16 (over z, x_lo).
Axes of the slice: x: 4 (x_hi: 2, x_lo: 2; x = x_hi * 2 + x_lo), y: 8, z: 8, core: 2. Of those that a mesh axis runs over, the one named last changes fastest.
Arguments:
- psi: float32 [512, 192, 512], P('band', 'dom'), may hold values from -40 to 40, as said below
- potential: float32 [192, 512], P('dom'), may hold values from -3 to 1
Outputs:
- filtered_basis: float32 [512, 192, 512], P('band', 'dom')
Inputs may be any that keep to these rules, and one draw needn't show every extreme that they name: `psi`: real-valued band functions.
All inputs are finite; a program needn't handle non-finite values.
Results may differ from a plain program's by a relative error of at most 0.0002.
Values sent between devices are 32-bit elements; how exact they have to be, the bound alone decides.
No kernel may reach another device: no remote copies, remote signals or barrier semaphores. Data moves between devices by JAX's collectives and lax.ppermute only.
A program may use at most 64 MiB of HBM per device.

v0:
```python
import jax
import jax.numpy as jnp
from jax import lax
from jax.sharding import PartitionSpec as P

LX = 32
DEG = 4
COEF = (
    -5369.0 / 1800.0,
    12.0 / 7.0,
    -15.0 / 56.0,
    10.0 / 189.0,
    -1.0 / 112.0,
    2.0 / 1925.0,
    -1.0 / 16632.0,
)
INV_SPACING2 = 4.0
CENTRE = 24.0
HALF_WIDTH = 20.0


def with_halo(block, sides, width):
    for axis, dim in sides:
        count = lax.axis_size(axis)
        forward = [(i, i + 1) for i in range(count - 1)]
        backward = [(target, source) for source, target in forward]
        low = lax.ppermute(
            lax.slice_in_dim(block, block.shape[dim] - width, None, axis=dim), axis, forward
        )
        high = lax.ppermute(lax.slice_in_dim(block, 0, width, axis=dim), axis, backward)
        block = jnp.concatenate([low, block, high], axis=dim)
    return block


def shift_x(values, step):
    amount = step % LX
    column = lax.broadcasted_iota(jnp.int32, values.shape, 2) % LX
    return jnp.where(
        column >= amount, jnp.roll(values, amount, 2), jnp.roll(values, amount - LX, 2)
    )


def shift_y(values, step):
    return jnp.roll(values, step * LX, 2)


def hamiltonian(values, potential):
    depth = values.shape[1]
    padded = with_halo(values, (("dom", 1),), 6)
    summed = 3.0 * COEF[0] * values
    for step in range(1, 7):
        beside_all = shift_x(values, step) + shift_x(values, -step)
        beside_all = beside_all + shift_y(values, step) + shift_y(values, -step)
        beside_all = (
            beside_all
            + padded[:, 6 + step : 6 + step + depth]
            + padded[:, 6 - step : 6 - step + depth]
        )
        summed = summed + COEF[step] * beside_all
    return -0.5 * INV_SPACING2 * summed + potential[None] * values


def chebyshev(start, potential):
    previous = start
    current = (hamiltonian(start, potential) - CENTRE * start) / HALF_WIDTH
    for degree in range(1, DEG):
        following = (
            2.0 * (hamiltonian(current, potential) - CENTRE * current) / HALF_WIDTH - previous
        )
        previous, current = (current, following)
    return current


def inverse_rows(gram, all_bands, tile_bands):
    lower = jnp.linalg.cholesky(gram)
    inverse = lax.linalg.triangular_solve(
        lower, jnp.eye(all_bands, dtype=jnp.float32), left_side=True, lower=True
    )
    return lax.dynamic_slice_in_dim(inverse, lax.axis_index("band") * tile_bands, tile_bands, 0)


def shards(psi, potential):
    filtered = chebyshev(psi, potential)
    tile_bands = psi.shape[0]
    points_dev = psi.shape[1] * psi.shape[2]
    all_points = points_dev * lax.axis_size("dom")
    all_bands = tile_bands * lax.axis_size("band")
    flatrows = filtered.reshape(tile_bands, points_dev)
    piece = lax.all_gather(filtered, "band", axis=0, tiled=True)
    count = piece.shape[0]
    contrib = jnp.dot(
        flatrows,
        piece.reshape(count, points_dev).T,
        precision=lax.Precision.HIGHEST,
        preferred_element_type=jnp.float32,
    )
    gram_rows = lax.psum(contrib, "dom") / all_points
    gram = lax.all_gather(gram_rows, "band", axis=0, tiled=True)
    my_rows = inverse_rows(gram, all_bands, tile_bands)
    piece = lax.all_gather(filtered, "band", axis=0, tiled=True)
    count = piece.shape[0]
    rotated = jnp.dot(
        my_rows,
        piece.reshape(count, points_dev),
        precision=lax.Precision.HIGHEST,
        preferred_element_type=jnp.float32,
    )
    return rotated.reshape(psi.shape)


def solution(mesh):
    placed = (P("band", "dom", None), P("dom", None))
    return jax.shard_map(
        shards, mesh=mesh, in_specs=placed, out_specs=P("band", "dom", None), check_vma=False
    )
```

profile of v0, /device:TPU:6, one launch (start us, length us, event | category | flops | bytes accessed | tf_op | source)
XLA Modules:
  0.0 725.2 jit_solution(7436480236359161126)
XLA Ops:
  8.6 5.1 collective-permute-start
  23.2 3.9 broadcast_multiply_fusion
  38.7 8.4 %collective-permute-done.3 = f32[32,6,512]{2,0,1:T(8,128)S(1)} collective-permute-done((f32[32,6,512]{2,0,1:T(8,128)S(1)}, f32[32,6,512]{2,0,1:T(8,128)S(1)}, u32[]{:S(2)}, u32[]{:S(2)}) %collective-permute-start.3) | collective-permute-done | bytes 393248 | tf_op jit(solution)/shard_map/ppermute | solution.py:27
  47.1 3.8 fusion.80
  60.9 6.2 collective-permute-done.5
  67.1 3.8 fusion.92
  75.7 2.8 collective-permute-start.7
  80.9 6.3 collective-permute-done.7
  87.3 4.5 fusion.104
  91.8 150.9 %all-gather.3.cloned.1.call-done = f32[512,6,512]{2,0,1:T(8,128)} async-done(((f32[32,6,512]{2,0,1:T(8,128)}), f32[512,6,512]{2,0,1:T(8,128)}) %all-gather.3.cloned.1.call-update) | async-done | bytes 6291472 | tf_op jit(solution)/shard_map/all_gather | solution.py:89
  242.7 9.3 %convolution_bitcast_fusion = f32[32,512]{1,0:T(8,128)} fusion(f32[32,6,512]{2,0,1:T(8,128)} %fusion.104, f32[512,6,512]{2,0,1:T(8,128)} %all-gather.3.cloned.1.call-done), kind=kOutput, calls=%fused_computation.72 | convolution fusion | flops 603979776 | bytes 6750208 | tf_op jit(solution)/shard_map/dot_general | solution.py:91
  252.0 242.1 %all-reduce.3.cloned.1.call-done = f32[32,512]{1,0:T(8,128)} async-done(((f32[32,512]{1,0:T(8,128)}), f32[32,512]{1,0:T(8,128)}) %all-reduce.3.cloned.1.call-update) | async-done | bytes 65552 | tf_op jit(solution)/shard_map/psum | solution.py:97
  496.6 6.7 copy.9
  503.3 65.1 %all-gather.5.cloned.1.call-done = f32[512,512]{1,0:T(8,128)} async-done(((f32[32,512]{1,0:T(8,128)}), f32[512,512]{1,0:T(8,128)}) %all-gather.5.cloned.1.call-update) | async-done | bytes 1048592 | tf_op jit(solution)/shard_map/all_gather | solution.py:98
  571.4 11.7 %cholesky.104 = f32[128,128]{1,0:T(8,128)S(1)} custom-call(f32[128,128]{1,0:T(8,128)S(1)} %cholesky.266), custom_call_target="Cholesky" | custom-call | tf_op jit(solution)/shard_map/jit(cholesky)/cholesky | solution.py:75
  583.3 9.8 %custom-call.30 = f32[1,128,128]{1,2,0:T(8,128)S(1)} custom-call(f32[1,128,128]{2,1,0:T(8,128)S(1)} %get-tuple-element.324), custom_call_target="InvertDiagBlocksLowerTriangular" | custom-call | tf_op jit(solution)/shard_map/jit(cholesky)/cholesky | solution.py:75
  593.8 11.7 %cholesky.217 = f32[128,128]{1,0:T(8,128)S(1)} custom-call(f32[128,128]{1,0:T(8,128)S(1)} %cholesky.270), custom_call_target="Cholesky" | custom-call | tf_op jit(solution)/shard_map/jit(cholesky)/cholesky | solution.py:75
  605.5 10.0 %custom-call.31 = f32[1,128,128]{1,2,0:T(8,128)S(1)} custom-call(f32[1,128,128]{2,1,0:T(8,128)S(1)} %get-tuple-element.321), custom_call_target="InvertDiagBlocksLowerTriangular" | custom-call | tf_op jit(solution)/shard_map/jit(cholesky)/cholesky | solution.py:75
  616.2 11.7 %cholesky.238 = f32[128,128]{1,0:T(8,128)S(1)} custom-call(f32[128,128]{1,0:T(8,128)S(1)} %cholesky.275), custom_call_target="Cholesky" | custom-call | tf_op jit(solution)/shard_map/jit(cholesky)/cholesky | solution.py:75
  628.5 9.8 %custom-call.32 = f32[1,128,128]{1,2,0:T(8,128)S(1)} custom-call(f32[1,128,128]{2,1,0:T(8,128)S(1)} %get-tuple-element.318), custom_call_target="InvertDiagBlocksLowerTriangular" | custom-call | tf_op jit(solution)/shard_map/jit(cholesky)/cholesky | solution.py:75
  639.0 11.7 %cholesky.255 = f32[128,128]{1,0:T(8,128)S(1)} custom-call(f32[128,128]{1,0:T(8,128)S(1)} %convolution_subtract_fusion.5), custom_call_target="Cholesky" | custom-call | tf_op jit(solution)/shard_map/jit(cholesky)/cholesky | solution.py:75
  654.7 10.3 %while.1 = (s32[]{:T(128)}, f32[512,512]{1,0:T(8,128)S(1)}, s32[4,2]{0,1:T(2,128)S(1)}, f32[4,128,128]{2,1,0:T(8,128)}, s32[]{:T(128)}) while((s32[]{:T(128)}, f32[512,512]{1,0:T(8,128)S(1)}, s32[4,2]{0,1:T(2,128)S(1)}, f32[4,128,128]{2,1,0:T(8,128)}, s32[]{:T(128)}) %tuple.173), condition=%wide.while_cond, body=%wide.while_body.sunk | while | flops 2 | bytes 132705 | solution.py:76
  665.0 40.1 %custom-call.33 = f32[4,128,128]{1,2,0:T(8,128)S(1)} custom-call(f32[4,128,128]{2,1,0:T(8,128)} %get-tuple-element.12), custom_call_target="InvertDiagBlocksLowerTriangular" | custom-call | tf_op jit(solution)/shard_map/triangular_solve | solution.py:76
  709.0 9.2 %fusion = f32[32,6,512]{2,0,1:T(8,128)} fusion(f32[512,6,512]{0,2,1:T(8,128)} %copy.9, s32[]{:T(128)S(6)} %select_n.397, f32[128,512]{1,0:T(8,128)S(1)} %fusion.271, f32[128,512]{1,0:T(8,128)S(1)} %fusion.286, f32[128,512]{1,0:T(8,128)S(1)} %fusion.284, f32[128,512]{1,0:T(8,128)S(1)} %fusion.283), kind=kOutput, calls=%fused_computation.2 | convolution fusion | flops 604028928 | bytes 7733252 | tf_op jit(solution)/shard_map/dot_general | solution.py:102
  (217 shorter events, 63.2 us)
Async XLA Ops:
  6.5 12.4 %copy-start = (f32[32,6,512]{2,0,1:T(8,128)S(1)}, f32[32,6,512]{2,0,1:T(8,128)}, u32[]{:S(2)}) copy-start(f32[32,6,512]{2,0,1:T(8,128)} %param.2) | copy-start | bytes 1179652
  6.5 236.2 %all-gather.3.cloned.1.call-start = ((), (), s32[]{:S(2)}) async-start(), calls=%async_computation | async-start | bytes 6684672 | tf_op jit(solution)/shard_map/all_gather | solution.py:89
  6.5 16.4 %collective-permute-start.1 = (f32[32,6,512]{2,0,1:T(8,128)}, f32[32,6,512]{2,0,1:T(8,128)S(1)}, u32[]{:S(2)}, u32[]{:S(2)}) collective-permute-start(f32[32,6,512]{2,0,1:T(8,128)} %param.2), channel_id=1, source_target_pairs={{0,16},{16,32},{32,48},{48,64},{64,80},{80,96},{96,112},{112,128},... | collective-permute-start | bytes 1179656 | tf_op jit(solution)/shard_map/ppermute | solution.py:27
  8.6 14.5 %collective-permute-start = (f32[32,6,512]{2,0,1:T(8,128)}, f32[32,6,512]{2,0,1:T(8,128)S(1)}, u32[]{:S(2)}, u32[]{:S(2)}) collective-permute-start(f32[32,6,512]{2,0,1:T(8,128)} %param.2), channel_id=1, source_target_pairs={{16,0},{32,16},{48,32},{64,48},{80,64},{96,80},{112,96},{128,112},... | collective-permute-start | bytes 1179656 | tf_op jit(solution)/shard_map/ppermute | solution.py:30
  20.7 2.2 copy-start.1
  31.5 7.2 collective-permute-start.2
  33.4 13.7 %collective-permute-start.3 = (f32[32,6,512]{2,0,1:T(8,128)S(1)}, f32[32,6,512]{2,0,1:T(8,128)S(1)}, u32[]{:S(2)}, u32[]{:S(2)}) collective-permute-start(f32[32,6,512]{2,0,1:T(8,128)S(1)} %get-tuple-element.21), channel_id=1, source_target_pairs={{0,16},{16,32},{32,48},{48,64},{64,80},{80,96},{96,112},{112,128},... | collective-permute-start | bytes 1179656 | tf_op jit(solution)/shard_map/ppermute | solution.py:27
  53.7 7.2 collective-permute-start.4
  55.6 11.5 %collective-permute-start.5 = (f32[32,6,512]{2,0,1:T(8,128)S(1)}, f32[32,6,512]{2,0,1:T(8,128)S(1)}, u32[]{:S(2)}, u32[]{:S(2)}) collective-permute-start(f32[32,6,512]{2,0,1:T(8,128)S(1)} %fusion.80), channel_id=1, source_target_pairs={{0,16},{16,32},{32,48},{48,64},{64,80},{80,96},{96,112},{112,128},... | collective-permute-start | bytes 1179656 | tf_op jit(solution)/shard_map/ppermute | solution.py:27
  73.7 7.2 collective-permute-start.6
  75.7 11.6 %collective-permute-start.7 = (f32[32,6,512]{2,0,1:T(8,128)S(1)}, f32[32,6,512]{2,0,1:T(8,128)S(1)}, u32[]{:S(2)}, u32[]{:S(2)}) collective-permute-start(f32[32,6,512]{2,0,1:T(8,128)S(1)} %fusion.92), channel_id=1, source_target_pairs={{0,16},{16,32},{32,48},{48,64},{64,80},{80,96},{96,112},{112,128},... | collective-permute-start | bytes 1179656 | tf_op jit(solution)/shard_map/ppermute | solution.py:27
  91.7 402.4 %all-reduce.3.cloned.1.call-start = ((), (), s32[]{:S(2)}) async-start(), calls=%async_computation.1 | async-start | bytes 131072 | tf_op jit(solution)/shard_map/psum | solution.py:97
  252.0 316.4 %all-gather.5.cloned.1.call-start = ((), (), s32[]{:S(2)}) async-start(), calls=%async_computation.2 | async-start | bytes 1114112 | tf_op jit(solution)/shard_map/all_gather | solution.py:98
Sparse Core Ops, SparseCore 0:
  91.9 150.8 all-gather.2
  252.1 241.9 all-reduce.2
  496.2 72.0 all-gather.4
where the time goes:
time: 732 us; the launch traced here: 725 us
  waiting for transfers between devices  483 us (66%)
  other arithmetic  139 us (19%)
  local copies, waits for them, and re-layouts  41.3 us (6%)
  matrix products  24.1 us (3%)
  starting transfers between devices  20.9 us (3%)
  between operations  17 us (2%)
    psum x1, waiting for transfers between devices, shards(): gram_rows = lax.psum(contrib, 'dom') / all_points  242 us
    all_gather x1, waiting for transfers between devices, shards(): piece = lax.all_gather(filtered, 'band', axis=0, tiled=True)  151 us
    another operation x14, other arithmetic, inverse_rows(): lower = jnp.linalg.cholesky(gram)  78.6 us
    all_gather x1, waiting for transfers between devices, shards(): gram = lax.all_gather(gram_rows, 'band', axis=0, tiled=True)  65.1 us
    another operation x3, other arithmetic, inverse_rows(): lax.linalg.triangular_solve(lower, jnp.eye(all_bands, dtype=jnp.float32),...  40.3 us
    ppermute x4, waiting for transfers between devices, with_halo(): lax.ppermute(lax.slice_in_dim(block, block.shape[dim] - width, None, axis...  20.9 us
  transfers between devices with their start and end apart: 11, of which 9 were waited for; matrix products, arithmetic and copies ran while one was open for 3% of the time, Pallas kernels for 0%

commit v1 on v0

--- a/solution.py
+++ b/solution.py
@@ -17,6 +17,11 @@
 INV_SPACING2 = 4.0
 CENTRE = 24.0
 HALF_WIDTH = 20.0
+
+
+def _obtain_racks(net_axis, point):
+    row_out = jnp.sum(jax.lax.all_gather(point, net_axis), axis=0)
+    return row_out
 
 
 def with_halo(block, sides, width):
@@ -94,7 +99,7 @@
         precision=lax.Precision.HIGHEST,
         preferred_element_type=jnp.float32,
     )
-    gram_rows = lax.psum(contrib, "dom") / all_points
+    gram_rows = _obtain_racks("dom", contrib) / all_points
     gram = lax.all_gather(gram_rows, "band", axis=0, tiled=True)
     my_rows = inverse_rows(gram, all_bands, tile_bands)
     piece = lax.all_gather(filtered, "band", axis=0, tiled=True)

time: 732 us -> 573 us (0.78)
  waiting for transfers between devices: 483 us -> 324 us
    psum x1 -> x0, waiting for transfers between devices: 242 us -> none  [shards(): gram_rows = lax.psum(contrib, 'dom') / all_points]
    all_gather x0 -> x1, waiting for transfers between devices: none -> 84.9 us  [_obtain_racks(): row_out = jnp.sum(jax.lax.all_gather(point, net_axis), axis=0)]
  transfers between devices with their start and end apart: 11 -> 11, of which waited for: 9 -> 9; matrix products, arithmetic and copies ran while one was open for 3% -> 4% of each run, Pallas kernels for 0% -> 0%
where the time goes in v1:
time: 573 us; the launch traced here: 567 us
  waiting for transfers between devices  324 us (57%)
  other arithmetic  139 us (24%)
  local copies, waits for them, and re-layouts  41.3 us (7%)
  matrix products  24.1 us (4%)
  starting transfers between devices  20.9 us (4%)
  between operations  17 us (3%)
    all_gather x1, waiting for transfers between devices, shards(): piece = lax.all_gather(filtered, 'band', axis=0, tiled=True)  151 us
    all_gather x1, waiting for transfers between devices, _obtain_racks(): row_out = jnp.sum(jax.lax.all_gather(point, net_axis), axis=0)  84.9 us
    another operation x14, other arithmetic, inverse_rows(): lower = jnp.linalg.cholesky(gram)  78.6 us
    all_gather x1, waiting for transfers between devices, shards(): gram = lax.all_gather(gram_rows, 'band', axis=0, tiled=True)  62.8 us
    another operation x3, other arithmetic, inverse_rows(): lax.linalg.triangular_solve(lower, jnp.eye(all_bands, dtype=jnp.float32),...  40.3 us
    ppermute x4, waiting for transfers between devices, with_halo(): lax.ppermute(lax.slice_in_dim(block, block.shape[dim] - width, None, axis...  20.9 us
    sub x3, other arithmetic, chebyshev(): 2.0 * (hamiltonian(current, potential) - CENTRE * current) / HALF_WIDTH  12 us
  transfers between devices with their start and end apart: 11, of which 9 were waited for; matrix products, arithmetic and copies ran while one was open for 4% of the time, Pallas kernels for 0%

profile of v1, /device:TPU:6, one launch (start us, length us, event | category | flops | bytes accessed | tf_op | source)
XLA Modules:
  0.0 566.7 jit_solution(12525462955464050669)
XLA Ops:
  8.6 5.1 collective-permute-start
  23.2 3.9 broadcast_multiply_fusion
  38.7 8.4 %collective-permute-done.3 = f32[32,6,512]{2,0,1:T(8,128)S(1)} collective-permute-done((f32[32,6,512]{2,0,1:T(8,128)S(1)}, f32[32,6,512]{2,0,1:T(8,128)S(1)}, u32[]{:S(2)}, u32[]{:S(2)}) %collective-permute-start.3) | collective-permute-done | bytes 393248 | tf_op jit(solution)/shard_map/ppermute | solution.py:32
  47.1 3.8 fusion.80
  60.9 6.2 %collective-permute-done.5 = f32[32,6,512]{2,0,1:T(8,128)S(1)} collective-permute-done((f32[32,6,512]{2,0,1:T(8,128)S(1)}, f32[32,6,512]{2,0,1:T(8,128)S(1)}, u32[]{:S(2)}, u32[]{:S(2)}) %collective-permute-start.5) | collective-permute-done | bytes 393248 | tf_op jit(solution)/shard_map/ppermute | solution.py:32
  67.1 3.8 fusion.92
  75.7 2.8 collective-permute-start.7
  80.9 6.3 %collective-permute-done.7 = f32[32,6,512]{2,0,1:T(8,128)S(1)} collective-permute-done((f32[32,6,512]{2,0,1:T(8,128)S(1)}, f32[32,6,512]{2,0,1:T(8,128)S(1)}, u32[]{:S(2)}, u32[]{:S(2)}) %collective-permute-start.7) | collective-permute-done | bytes 393248 | tf_op jit(solution)/shard_map/ppermute | solution.py:32
  87.3 4.5 fusion.104
  91.8 150.9 %all-gather.5.cloned.1.call-done = f32[512,6,512]{2,0,1:T(8,128)} async-done(((f32[32,6,512]{2,0,1:T(8,128)}), f32[512,6,512]{2,0,1:T(8,128)}) %all-gather.5.cloned.1.call-update) | async-done | bytes 6291472 | tf_op jit(solution)/shard_map/all_gather | solution.py:94
  242.7 9.3 %convolution_bitcast_fusion = f32[32,512]{1,0:T(8,128)} fusion(f32[32,6,512]{2,0,1:T(8,128)} %fusion.104, f32[512,6,512]{2,0,1:T(8,128)} %all-gather.5.cloned.1.call-done), kind=kOutput, calls=%fused_computation.72 | convolution fusion | flops 603979776 | bytes 6750208 | tf_op jit(solution)/shard_map/dot_general | solution.py:96
  252.1 84.9 %all-gather.9.cloned.1.call-done = f32[1024,512]{1,0:T(8,128)} async-done(((f32[32,512]{1,0:T(8,128)}), f32[1024,512]{1,0:T(8,128)}) %all-gather.9.cloned.1.call-update) | async-done | bytes 2097168 | tf_op jit(solution)/shard_map/all_gather | solution.py:23
  340.3 6.7 %copy.7 = f32[512,6,512]{0,2,1:T(8,128)} copy(f32[512,6,512]{2,0,1:T(8,128)} %all-gather.5.cloned.1.call-done) | data formatting | bytes 12582912 | tf_op jit(solution)/shard_map/all_gather | solution.py:94
  347.0 62.8 %all-gather.7.cloned.1.call-done = f32[512,512]{1,0:T(8,128)} async-done(((f32[32,512]{1,0:T(8,128)}), f32[512,512]{1,0:T(8,128)}) %all-gather.7.cloned.1.call-update) | async-done | bytes 1048592 | tf_op jit(solution)/shard_map/all_gather | solution.py:103
  412.9 11.7 %cholesky.104 = f32[128,128]{1,0:T(8,128)S(1)} custom-call(f32[128,128]{1,0:T(8,128)S(1)} %cholesky.266), custom_call_target="Cholesky" | custom-call | tf_op jit(solution)/shard_map/jit(cholesky)/cholesky | solution.py:80
  424.7 9.8 %custom-call.30 = f32[1,128,128]{1,2,0:T(8,128)S(1)} custom-call(f32[1,128,128]{2,1,0:T(8,128)S(1)} %get-tuple-element.324), custom_call_target="InvertDiagBlocksLowerTriangular" | custom-call | tf_op jit(solution)/shard_map/jit(cholesky)/cholesky | solution.py:80
  435.2 11.7 %cholesky.217 = f32[128,128]{1,0:T(8,128)S(1)} custom-call(f32[128,128]{1,0:T(8,128)S(1)} %cholesky.270), custom_call_target="Cholesky" | custom-call | tf_op jit(solution)/shard_map/jit(cholesky)/cholesky | solution.py:80
  447.0 10.0 %custom-call.31 = f32[1,128,128]{1,2,0:T(8,128)S(1)} custom-call(f32[1,128,128]{2,1,0:T(8,128)S(1)} %get-tuple-element.321), custom_call_target="InvertDiagBlocksLowerTriangular" | custom-call | tf_op jit(solution)/shard_map/jit(cholesky)/cholesky | solution.py:80
  457.6 11.7 %cholesky.238 = f32[128,128]{1,0:T(8,128)S(1)} custom-call(f32[128,128]{1,0:T(8,128)S(1)} %cholesky.275), custom_call_target="Cholesky" | custom-call | tf_op jit(solution)/shard_map/jit(cholesky)/cholesky | solution.py:80
  470.0 9.8 %custom-call.32 = f32[1,128,128]{1,2,0:T(8,128)S(1)} custom-call(f32[1,128,128]{2,1,0:T(8,128)S(1)} %get-tuple-element.318), custom_call_target="InvertDiagBlocksLowerTriangular" | custom-call | tf_op jit(solution)/shard_map/jit(cholesky)/cholesky | solution.py:80
  480.4 11.7 %cholesky.255 = f32[128,128]{1,0:T(8,128)S(1)} custom-call(f32[128,128]{1,0:T(8,128)S(1)} %convolution_subtract_fusion.5), custom_call_target="Cholesky" | custom-call | tf_op jit(solution)/shard_map/jit(cholesky)/cholesky | solution.py:80
  496.2 10.3 %while.1 = (s32[]{:T(128)}, f32[512,512]{1,0:T(8,128)S(1)}, s32[4,2]{0,1:T(2,128)S(1)}, f32[4,128,128]{2,1,0:T(8,128)}, s32[]{:T(128)}) while((s32[]{:T(128)}, f32[512,512]{1,0:T(8,128)S(1)}, s32[4,2]{0,1:T(2,128)S(1)}, f32[4,128,128]{2,1,0:T(8,128)}, s32[]{:T(128)}) %tuple.173), condition=%wide.while_cond, body=%wide.while_body.sunk | while | flops 2 | bytes 132705 | solution.py:81
  506.5 40.1 %custom-call.33 = f32[4,128,128]{1,2,0:T(8,128)S(1)} custom-call(f32[4,128,128]{2,1,0:T(8,128)} %get-tuple-element.12), custom_call_target="InvertDiagBlocksLowerTriangular" | custom-call | tf_op jit(solution)/shard_map/triangular_solve | solution.py:81
  550.5 9.2 %fusion = f32[32,6,512]{2,0,1:T(8,128)} fusion(f32[512,6,512]{0,2,1:T(8,128)} %copy.7, s32[]{:T(128)S(6)} %select_n.397, f32[128,512]{1,0:T(8,128)S(1)} %fusion.271, f32[128,512]{1,0:T(8,128)S(1)} %fusion.286, f32[128,512]{1,0:T(8,128)S(1)} %fusion.284, f32[128,512]{1,0:T(8,128)S(1)} %fusion.283), kind=kOutput, calls=%fused_computation.2 | convolution fusion | flops 604028928 | bytes 7733252 | tf_op jit(solution)/shard_map/dot_general | solution.py:107
  (218 shorter events, 64.1 us)
Async XLA Ops:
  6.5 12.4 %copy-start = (f32[32,6,512]{2,0,1:T(8,128)S(1)}, f32[32,6,512]{2,0,1:T(8,128)}, u32[]{:S(2)}) copy-start(f32[32,6,512]{2,0,1:T(8,128)} %param.2) | copy-start | bytes 1179652
  6.5 236.2 %all-gather.5.cloned.1.call-start = ((), (), s32[]{:S(2)}) async-start(), calls=%async_computation | async-start | bytes 6684672 | tf_op jit(solution)/shard_map/all_gather | solution.py:94
  6.5 16.4 %collective-permute-start.1 = (f32[32,6,512]{2,0,1:T(8,128)}, f32[32,6,512]{2,0,1:T(8,128)S(1)}, u32[]{:S(2)}, u32[]{:S(2)}) collective-permute-start(f32[32,6,512]{2,0,1:T(8,128)} %param.2), channel_id=1, source_target_pairs={{0,16},{16,32},{32,48},{48,64},{64,80},{80,96},{96,112},{112,128},... | collective-permute-start | bytes 1179656 | tf_op jit(solution)/shard_map/ppermute | solution.py:32
  8.6 14.5 %collective-permute-start = (f32[32,6,512]{2,0,1:T(8,128)}, f32[32,6,512]{2,0,1:T(8,128)S(1)}, u32[]{:S(2)}, u32[]{:S(2)}) collective-permute-start(f32[32,6,512]{2,0,1:T(8,128)} %param.2), channel_id=1, source_target_pairs={{16,0},{32,16},{48,32},{64,48},{80,64},{96,80},{112,96},{128,112},... | collective-permute-start | bytes 1179656 | tf_op jit(solution)/shard_map/ppermute | solution.py:35
  20.7 2.2 copy-start.1
  31.5 7.2 %collective-permute-start.2 = (f32[32,6,512]{2,0,1:T(8,128)S(1)}, f32[32,6,512]{2,0,1:T(8,128)S(1)}, u32[]{:S(2)}, u32[]{:S(2)}) collective-permute-start(f32[32,6,512]{2,0,1:T(8,128)S(1)} %get-tuple-element.21), channel_id=1, source_target_pairs={{16,0},{32,16},{48,32},{64,48},{80,64},{96,80},{112,96},{128,112},... | collective-permute-start | bytes 1179656 | tf_op jit(solution)/shard_map/ppermute | solution.py:35
  33.4 13.7 %collective-permute-start.3 = (f32[32,6,512]{2,0,1:T(8,128)S(1)}, f32[32,6,512]{2,0,1:T(8,128)S(1)}, u32[]{:S(2)}, u32[]{:S(2)}) collective-permute-start(f32[32,6,512]{2,0,1:T(8,128)S(1)} %get-tuple-element.21), channel_id=1, source_target_pairs={{0,16},{16,32},{32,48},{48,64},{64,80},{80,96},{96,112},{112,128},... | collective-permute-start | bytes 1179656 | tf_op jit(solution)/shard_map/ppermute | solution.py:32
  53.7 7.2 %collective-permute-start.4 = (f32[32,6,512]{2,0,1:T(8,128)S(1)}, f32[32,6,512]{2,0,1:T(8,128)S(1)}, u32[]{:S(2)}, u32[]{:S(2)}) collective-permute-start(f32[32,6,512]{2,0,1:T(8,128)S(1)} %fusion.80), channel_id=1, source_target_pairs={{16,0},{32,16},{48,32},{64,48},{80,64},{96,80},{112,96},{128,112},... | collective-permute-start | bytes 1179656 | tf_op jit(solution)/shard_map/ppermute | solution.py:35
  55.6 11.5 %collective-permute-start.5 = (f32[32,6,512]{2,0,1:T(8,128)S(1)}, f32[32,6,512]{2,0,1:T(8,128)S(1)}, u32[]{:S(2)}, u32[]{:S(2)}) collective-permute-start(f32[32,6,512]{2,0,1:T(8,128)S(1)} %fusion.80), channel_id=1, source_target_pairs={{0,16},{16,32},{32,48},{48,64},{64,80},{80,96},{96,112},{112,128},... | collective-permute-start | bytes 1179656 | tf_op jit(solution)/shard_map/ppermute | solution.py:32
  73.7 7.2 %collective-permute-start.6 = (f32[32,6,512]{2,0,1:T(8,128)S(1)}, f32[32,6,512]{2,0,1:T(8,128)S(1)}, u32[]{:S(2)}, u32[]{:S(2)}) collective-permute-start(f32[32,6,512]{2,0,1:T(8,128)S(1)} %fusion.92), channel_id=1, source_target_pairs={{16,0},{32,16},{48,32},{64,48},{80,64},{96,80},{112,96},{128,112},... | collective-permute-start | bytes 1179656 | tf_op jit(solution)/shard_map/ppermute | solution.py:35
  75.7 11.6 %collective-permute-start.7 = (f32[32,6,512]{2,0,1:T(8,128)S(1)}, f32[32,6,512]{2,0,1:T(8,128)S(1)}, u32[]{:S(2)}, u32[]{:S(2)}) collective-permute-start(f32[32,6,512]{2,0,1:T(8,128)S(1)} %fusion.92), channel_id=1, source_target_pairs={{0,16},{16,32},{32,48},{48,64},{64,80},{80,96},{96,112},{112,128},... | collective-permute-start | bytes 1179656 | tf_op jit(solution)/shard_map/ppermute | solution.py:32
  91.7 245.2 %all-gather.9.cloned.1.call-start = ((), (), s32[]{:S(2)}) async-start(), calls=%async_computation.2 | async-start | bytes 2162688 | tf_op jit(solution)/shard_map/all_gather | solution.py:23
  252.0 157.8 %all-gather.7.cloned.1.call-start = ((), (), s32[]{:S(2)}) async-start(), calls=%async_computation.1 | async-start | bytes 1114112 | tf_op jit(solution)/shard_map/all_gather | solution.py:103
Sparse Core Ops, SparseCore 0:
  91.9 150.8 all-gather.4
  252.1 84.7 all-gather.8
  339.5 70.3 all-gather.6
